TPU v7x, 32 devices: a whole 2x2x4 slice. The times are simulated.
32 devices in a mesh: group: 4 (over y, x), slot: 8 (over z, core).
Axes of the slice: x: 2, y: 2, z: 4, core: 2. Of those that a mesh axis runs over, the one named last changes fastest.
Arguments:
- tokens: bfloat16 [4096, 2048], P(('group', 'slot')), may hold values from -6 to 6
- cotangent: bfloat16 [4096, 512], P(('group', 'slot')), may hold values from -0.59765625 to 0.59765625
- weight_halves: bfloat16 [32, 1024, 512], P(('group', 'slot')), may hold values from -0.125 to 0.125
- momentum_halves: bfloat16 [32, 1024, 512], P(('group', 'slot')), may hold values from -6 to 6
- old_map: int32 [4, 4], replicated, may hold values from 0 to 3, each once within a row
- new_map: int32 [4, 8], replicated, may hold values from 0 to 3, as said below
- row_ids: int32 [32, 128], P(('group', 'slot')), may hold values from 0 to 127
Outputs:
- projected: bfloat16 [4096, 512], P(('group', 'slot'))
Inputs may be any that keep to these rules, and one draw needn't show every extreme that they name: `old_map`: each row names each of the group's experts once. `new_map`: every expert is hosted by one to four new slots; among the experts of every owner group one is hosted by exactly four.
All inputs are finite; a program needn't handle non-finite values.
Results may differ from a plain program's by a relative error of at most 0.007.
Values may be sent and summed in bfloat16 or wider, within the bound.
No kernel may reach another device: no remote copies, remote signals or barrier semaphores. Data moves between devices by JAX's collectives and lax.ppermute only.
A program may use at most 64 MiB of HBM per device.

v0:
```python
import math
import jax
import jax.numpy as jnp
from jax import lax
from jax.sharding import PartitionSpec as P

ITERS = 2
coef_a = 3.4445
coef_b = -4.775
coef_c = 2.0315
momentum_rate = 0.95
step_scale = 0.01
gram_eps = 1e-06
contract_rows = (((0,), (0,)), ((), ()))


def swapped(shard, axis, stride):
    return lax.ppermute(shard, axis, [(i, i ^ 1 << stride) for i in range(lax.axis_size(axis))])


def pick_columns(token_block, which_half, slot_count):
    row_count, col_count = token_block.shape
    pieces_view = token_block.reshape(row_count, slot_count, 2, col_count // (2 * slot_count))
    chosen = lax.dynamic_index_in_dim(pieces_view, which_half, axis=2, keepdims=False)
    return chosen.reshape(row_count, col_count // 2)


def inner_gram(half_rows):
    return lax.dot_general(
        half_rows, half_rows, contract_rows, preferred_element_type=jnp.float32
    ).astype(jnp.bfloat16)


def make_polynomial(scaled):
    gram_bf = scaled.astype(jnp.bfloat16)
    square = jnp.dot(gram_bf, gram_bf, preferred_element_type=jnp.float32)
    return (coef_b * scaled + coef_c * square).astype(jnp.bfloat16)


def on_device(tokens, cotangent, weight_halves, momentum_halves, old_map, new_map, row_ids):
    slot_count = lax.axis_size("slot")
    host_count = slot_count // lax.axis_size("group")
    model_width = tokens.shape[1]
    hidden = cotangent.shape[1]
    half_index = lax.axis_index("slot") % 2
    group_id = lax.axis_index("group")
    outgoing = jnp.concatenate(
        [pick_columns(tokens, 1 - half_index, slot_count), cotangent], axis=1
    )
    incoming = swapped(outgoing, "slot", 0)
    own_term = lax.dot_general(
        pick_columns(tokens, half_index, slot_count),
        cotangent,
        contract_rows,
        preferred_element_type=jnp.float32,
    ).astype(jnp.bfloat16)
    peer_term = lax.dot_general(
        incoming[:, : model_width // 2],
        incoming[:, model_width // 2 :],
        contract_rows,
        preferred_element_type=jnp.float32,
    ).astype(jnp.bfloat16)
    gradient = own_term.astype(jnp.float32) + peer_term.astype(jnp.float32)
    current = (momentum_rate * momentum_halves[0].astype(jnp.float32) + gradient).astype(
        jnp.bfloat16
    )
    own_gram = inner_gram(current)
    for iteration in range(ITERS):
        peer_gram = swapped(own_gram, "slot", 0)
        gram_sum = own_gram.astype(jnp.float32) + peer_gram.astype(jnp.float32)
        if iteration == 0:
            norm_sq = jnp.trace(gram_sum) + gram_eps
            gram_sum = gram_sum / norm_sq
            factor = 1.0 / jnp.sqrt(norm_sq)
        else:
            factor = 1.0
        polynomial = make_polynomial(gram_sum)
        product = jnp.dot(current, polynomial, preferred_element_type=jnp.float32)
        current = (factor * (coef_a * current.astype(jnp.float32) + product)).astype(jnp.bfloat16)
        if iteration + 1 < ITERS:
            own_gram = inner_gram(current)
    renewed = (
        weight_halves[0].astype(jnp.float32)
        - step_scale * math.sqrt(model_width) * current.astype(jnp.float32)
    ).astype(jnp.bfloat16)
    blocks = lax.all_to_all(
        renewed.reshape(slot_count, -1, hidden), "slot", split_axis=0, concat_axis=0, tiled=True
    )
    pieces = blocks.reshape(slot_count // 2, -1, hidden)
    requests = lax.dynamic_slice_in_dim(new_map, group_id * host_count, host_count, axis=1).reshape(
        -1
    )
    own_list = lax.dynamic_index_in_dim(old_map, group_id, 0, keepdims=False)
    holder = jnp.argmax((own_list[None, :] == requests[:, None]).astype(jnp.int32), axis=1)
    outgoing_blocks = jnp.take(pieces, holder, axis=0)
    weight_new = lax.all_to_all(
        lax.all_to_all(outgoing_blocks, "group", split_axis=0, concat_axis=0, tiled=True),
        "slot",
        split_axis=0,
        concat_axis=1,
        tiled=True,
    )[0]
    chosen = jnp.take(tokens, row_ids[0], axis=0)
    return jnp.dot(chosen, weight_new, preferred_element_type=jnp.float32).astype(jnp.bfloat16)


def solution(mesh):
    placed = (
        P(("group", "slot"), None),
        P(("group", "slot"), None),
        P(("group", "slot"), None, None),
        P(("group", "slot"), None, None),
        P(),
        P(),
        P(("group", "slot"), None),
    )
    return jax.shard_map(
        on_device, mesh=mesh, in_specs=placed, out_specs=P(("group", "slot"), None), check_vma=False
    )
```

profile of v0, /device:TPU:0, one launch (start us, length us, event | category | flops | bytes accessed | tf_op | source)
XLA Modules:
  0.0 131.6 jit_solution(12882281342114190404)
XLA Ops:
  0.0 1.4 %copy.11 = bf16[128,2048]{0,1:T(8,128)(2,1)S(1)} copy(bf16[128,2048]{1,0:T(8,128)(2,1)} %param.7) | data formatting | bytes 1048576 | tf_op args[0]
  1.4 1.0 copy.12
  2.5 0.6 collective-permute-start
  3.5 0.9 collective-permute-done
  4.5 0.5 fusion.1
  5.0 0.7 convolution_convert_fusion.3
  5.7 0.4 collective-permute-start.1
  6.2 1.5 %collective-permute-done.1 = bf16[512,512]{1,0:T(8,128)(2,1)S(1)} collective-permute-done((bf16[512,512]{1,0:T(8,128)(2,1)S(1)}, bf16[512,512]{1,0:T(8,128)(2,1)S(1)}, u32[]{:S(2)}, u32[]{:S(2)}) %collective-permute-start.1) | collective-permute-done | bytes 524320 | tf_op jit(solution)/shard_map/ppermute | solution.py:18
  7.7 0.7 select_reduce_fusion
  9.1 1.2 multiply_convert_fusion
  10.3 0.7 convolution_convert_fusion.2
  11.0 0.4 collective-permute-start.2
  11.4 1.5 %collective-permute-done.2 = bf16[512,512]{1,0:T(8,128)(2,1)S(1)} collective-permute-done((bf16[512,512]{1,0:T(8,128)(2,1)S(1)}, bf16[512,512]{1,0:T(8,128)(2,1)S(1)}, u32[]{:S(2)}, u32[]{:S(2)}) %collective-permute-start.2) | collective-permute-done | bytes 524320 | tf_op jit(solution)/shard_map/ppermute | solution.py:18
  13.0 2.3 %fusion = bf16[1024,512]{1,0:T(8,128)(2,1)} fusion(bf16[1024,512]{1,0:T(8,128)(2,1)S(1)} %multiply_convert_fusion, bf16[1,1024,512]{2,1,0:T(8,128)(2,1)S(1)} %copy-done.4, bf16[512,512]{1,0:T(8,128)(2,1)S(1)} %collective-permute-done.2, bf16[512,512]{1,0:T(8,128)(2,1)S(1)} %convolution_convert_fusion.2), kind=kOutput, calls=%fused_computation.3 | convolution fusion | flops 812908544 | bytes 4194304 | tf_op jit(solution)/shard_map/dot_general | solution.py:78
  15.3 6.2 %all-to-all-start = ((bf16[8,128,512]{2,1,0:T(8,128)(2,1)}), bf16[8,128,512]{2,1,0:T(8,128)(2,1)S(1)}, u32[]{:S(2)}, u32[]{:S(2)}) async-start(bf16[8,128,512]{2,1,0:T(8,128)(2,1)} %bitcast.9), calls=%async_computation | async-start | bytes 2097152 | tf_op jit(solution)/shard_map/all_to_all | solution.py:86
  21.7 0.7 fusion.24
  22.3 0.6 iota_reduce_fusion
  23.0 25.1 %all-to-all-done = bf16[8,128,512]{2,1,0:T(8,128)(2,1)S(1)} async-done(((bf16[8,128,512]{2,1,0:T(8,128)(2,1)}), bf16[8,128,512]{2,1,0:T(8,128)(2,1)S(1)}, u32[]{:S(2)}, u32[]{:S(2)}) %all-to-all-start) | async-done | bytes 1048608 | tf_op jit(solution)/shard_map/all_to_all | solution.py:86
  48.0 0.7 gather_fusion.1
  49.0 28.7 %all_to_all.19 = bf16[8,256,512]{2,1,0:T(8,128)(2,1)} all-to-all(bf16[8,256,512]{2,1,0:T(8,128)(2,1)S(1)} %broadcast_select_fusion), channel_id=1, replica_groups=mesh['group'=4,'slot'=8] {'group'}, dimensions={0} | all-to-all | bytes 4194304 | tf_op jit(solution)/shard_map/all_to_all | solution.py:97
  77.7 3.7 %all-to-all-start.2 = ((bf16[8,256,512]{2,1,0:T(8,128)(2,1)}), bf16[8,256,512]{2,1,0:T(8,128)(2,1)S(1)}, u32[]{:S(2)}, u32[]{:S(2)}) async-start(bf16[8,256,512]{2,1,0:T(8,128)(2,1)} %all_to_all.19), calls=%async_computation.2 | async-start | bytes 4194304 | tf_op jit(solution)/shard_map/all_to_all | solution.py:96
  81.5 0.9 gather_fusion
  82.5 48.0 %all-to-all-done.2 = bf16[8,256,512]{2,1,0:T(8,128)(2,1)S(1)} async-done(((bf16[8,256,512]{2,1,0:T(8,128)(2,1)}), bf16[8,256,512]{2,1,0:T(8,128)(2,1)S(1)}, u32[]{:S(2)}, u32[]{:S(2)}) %all-to-all-start.2) | async-done | bytes 2097184 | tf_op jit(solution)/shard_map/all_to_all | solution.py:96
  130.4 1.1 convolution_convert_fusion.4
  (24 shorter events, 1.0 us)
Async XLA Ops:
  0.0 21.5 %copy-start = (s32[4,8]{1,0:T(4,128)S(1)}, s32[4,8]{1,0:T(4,128)}, u32[]{:S(2)}) copy-start(s32[4,8]{1,0:T(4,128)} %param.12) | copy-start | bytes 388
  0.0 3.1 %copy-start.3 = (bf16[128,512]{1,0:T(8,128)(2,1)S(1)}, bf16[128,512]{1,0:T(8,128)(2,1)}, u32[]{:S(2)}) copy-start(bf16[128,512]{1,0:T(8,128)(2,1)} %param.8) | copy-start | bytes 393220
  0.0 4.5 %copy-start.2 = (bf16[1,1024,512]{2,1,0:T(8,128)(2,1)S(1)}, bf16[1,1024,512]{2,1,0:T(8,128)(2,1)}, u32[]{:S(2)}) copy-start(bf16[1,1024,512]{2,1,0:T(8,128)(2,1)} %param.10) | copy-start | bytes 3145732
  2.5 1.9 %collective-permute-start = (bf16[128,1536]{0,1:T(8,128)(2,1)S(1)}, bf16[128,1536]{0,1:T(8,128)(2,1)S(1)}, u32[]{:S(2)}, u32[]{:S(2)}) collective-permute-start(bf16[128,1536]{0,1:T(8,128)(2,1)S(1)} %pad_maximum_fusion), channel_id=1, source_target_pairs={{0,1},{1,0},{2,3},{3,2},{4,5},{5,4},{6,7},{7,6},{8,9},{9,8},{10,11... | collective-permute-start | bytes 1179656 | tf_op jit(solution)/shard_map/ppermute | solution.py:18
  5.7 2.0 %collective-permute-start.1 = (bf16[512,512]{1,0:T(8,128)(2,1)S(1)}, bf16[512,512]{1,0:T(8,128)(2,1)S(1)}, u32[]{:S(2)}, u32[]{:S(2)}) collective-permute-start(bf16[512,512]{1,0:T(8,128)(2,1)S(1)} %convolution_convert_fusion.3), channel_id=1, source_target_pairs={{0,1},{1,0},{2,3},{3,2},{4,5},{5,4},{6,7},{7,6},{8,9},{9,8},{10,11... | collective-permute-start | bytes 1572872 | tf_op jit(solution)/shard_map/ppermute | solution.py:18
  10.3 2.7 %copy-start.4 = (bf16[1,1024,512]{2,1,0:T(8,128)(2,1)S(1)}, bf16[1,1024,512]{2,1,0:T(8,128)(2,1)}, u32[]{:S(2)}) copy-start(bf16[1,1024,512]{2,1,0:T(8,128)(2,1)} %param.9) | copy-start | bytes 3145732
  11.0 2.0 %collective-permute-start.2 = (bf16[512,512]{1,0:T(8,128)(2,1)S(1)}, bf16[512,512]{1,0:T(8,128)(2,1)S(1)}, u32[]{:S(2)}, u32[]{:S(2)}) collective-permute-start(bf16[512,512]{1,0:T(8,128)(2,1)S(1)} %convolution_convert_fusion.2), channel_id=1, source_target_pairs={{0,1},{1,0},{2,3},{3,2},{4,5},{5,4},{6,7},{7,6},{8,9},{9,8},{10,11... | collective-permute-start | bytes 1572872 | tf_op jit(solution)/shard_map/ppermute | solution.py:18
  15.3 32.8 %all-to-all-start = ((bf16[8,128,512]{2,1,0:T(8,128)(2,1)}), bf16[8,128,512]{2,1,0:T(8,128)(2,1)S(1)}, u32[]{:S(2)}, u32[]{:S(2)}) async-start(bf16[8,128,512]{2,1,0:T(8,128)(2,1)} %bitcast.9), calls=%async_computation | async-start | bytes 2097152 | tf_op jit(solution)/shard_map/all_to_all | solution.py:86
  77.7 3.7 %copy-start.5 = (s32[1,128]{1,0:T(1,128)S(1)}, s32[1,128]{1,0:T(1,128)}, u32[]{:S(2)}) copy-start(s32[1,128]{1,0:T(1,128)} %param.13) | copy-start | bytes 1540
  77.7 3.8 %copy-start.1 = (bf16[128,2048]{1,0:T(8,128)(2,1)S(1)}, bf16[128,2048]{1,0:T(8,128)(2,1)}, u32[]{:S(2)}) copy-start(bf16[128,2048]{1,0:T(8,128)(2,1)} %param.7) | copy-start | bytes 1572868
  77.7 52.7 %all-to-all-start.2 = ((bf16[8,256,512]{2,1,0:T(8,128)(2,1)}), bf16[8,256,512]{2,1,0:T(8,128)(2,1)S(1)}, u32[]{:S(2)}, u32[]{:S(2)}) async-start(bf16[8,256,512]{2,1,0:T(8,128)(2,1)} %all_to_all.19), calls=%async_computation.2 | async-start | bytes 4194304 | tf_op jit(solution)/shard_map/all_to_all | solution.py:96
where the time goes:
time: 132 us
  waiting for transfers between devices  77.1 us (58%)
  blocking collectives  28.7 us (22%)
  starting transfers between devices  11.4 us (9%)
  matrix products  7.01 us (5%)
  local copies, waits for them, and re-layouts  4.96 us (4%)
  other arithmetic  1.6 us (1%)
    all_to_all x1, waiting for transfers between devices, on_device(): lax.all_to_all(lax.all_to_all(outgoing_blocks, 'group', split_axis=0, con...  48 us
    all_to_all x1, blocking collectives, on_device(): lax.all_to_all(outgoing_blocks, 'group', split_axis=0, concat_axis=0, til...  28.7 us
    all_to_all x1, waiting for transfers between devices, on_device(): lax.all_to_all(renewed.reshape(slot_count, -1, hidden), 'slot', split_axi...  25.1 us
    all_to_all x1, starting transfers between devices, on_device(): lax.all_to_all(renewed.reshape(slot_count, -1, hidden), 'slot', split_axi...  6.22 us
    ppermute x3, waiting for transfers between devices, swapped(): lax.ppermute(shard, axis, [(i, i ^ 1 << stride) for i in range(lax.axis_s...  4.01 us
    all_to_all x1, starting transfers between devices, on_device(): lax.all_to_all(lax.all_to_all(outgoing_blocks, 'group', split_axis=0, con...  3.73 us
    dot_general x2, matrix products, on_device(): product = jnp.dot(current, polynomial, preferred_element_type=jnp.float32)  3.44 us
  transfers between devices with their start and end apart: 5, of which 5 were waited for; matrix products, arithmetic and copies ran while one was open for 2% of the time, Pallas kernels for 0%

commit v1 on v0

--- a/solution.py
+++ b/solution.py
@@ -93,12 +93,22 @@
     own_list = lax.dynamic_index_in_dim(old_map, group_id, 0, keepdims=False)
     holder = jnp.argmax((own_list[None, :] == requests[:, None]).astype(jnp.int32), axis=1)
     outgoing_blocks = jnp.take(pieces, holder, axis=0)
-    weight_new = lax.all_to_all(
-        lax.all_to_all(outgoing_blocks, "group", split_axis=0, concat_axis=0, tiled=True),
-        "slot",
-        split_axis=0,
-        concat_axis=1,
-        tiled=True,
+    weight_new = jnp.concatenate(
+        lax.all_to_all(
+            jnp.stack(
+                jnp.split(
+                    lax.all_to_all(
+                        outgoing_blocks, "group", split_axis=0, concat_axis=0, tiled=True
+                    ),
+                    lax.axis_size("slot"),
+                    axis=0,
+                )
+            ),
+            "slot",
+            0,
+            0,
+        ),
+        axis=1,
     )[0]
     chosen = jnp.take(tokens, row_ids[0], axis=0)
     return jnp.dot(chosen, weight_new, preferred_element_type=jnp.float32).astype(jnp.bfloat16)

time: 132 us -> 138 us (1.045)
  local copies, waits for them, and re-layouts: 4.96 us -> 10.7 us
    unnamed x14 -> x21, local copies, waits for them, and re-layouts: 2.46 us -> 7.5 us
where the time goes in v1:
time: 138 us; the launch traced here: 137 us
  waiting for transfers between devices  77.1 us (56%)
  blocking collectives  28.6 us (21%)
  starting transfers between devices  11.4 us (8%)
  local copies, waits for them, and re-layouts  10.7 us (8%)
  matrix products  7.02 us (5%)
  other arithmetic  1.6 us (1%)
    all_to_all x1, waiting for transfers between devices, on_device(): lax.all_to_all(jnp.stack(jnp.split(lax.all_to_all(outgoing_blocks, 'group...  48 us
    all_to_all x1, blocking collectives, on_device(): lax.all_to_all(outgoing_blocks, 'group', split_axis=0, concat_axis=0, til...  28.6 us
    all_to_all x1, waiting for transfers between devices, on_device(): lax.all_to_all(renewed.reshape(slot_count, -1, hidden), 'slot', split_axi...  25.1 us
    unnamed x21, local copies, waits for them, and re-layouts  7.5 us
    all_to_all x1, starting transfers between devices, on_device(): lax.all_to_all(renewed.reshape(slot_count, -1, hidden), 'slot', split_axi...  6.22 us
    ppermute x3, waiting for transfers between devices, swapped(): lax.ppermute(shard, axis, [(i, i ^ 1 << stride) for i in range(lax.axis_s...  4.01 us
    all_to_all x1, starting transfers between devices, on_device(): lax.all_to_all(jnp.stack(jnp.split(lax.all_to_all(outgoing_blocks, 'group...  3.73 us
    dot_general x2, matrix products, on_device(): product = jnp.dot(current, polynomial, preferred_element_type=jnp.float32)  3.44 us
  transfers between devices with their start and end apart: 5, of which 5 were waited for; matrix products, arithmetic and copies ran while one was open for 2% of the time, Pallas kernels for 0%

profile of v1, /device:TPU:0, one launch (start us, length us, event | category | flops | bytes accessed | tf_op | source)
XLA Modules:
  0.0 137.2 jit_solution(13862555449779576536)
XLA Ops:
  0.0 1.4 %copy.11 = bf16[128,2048]{0,1:T(8,128)(2,1)S(1)} copy(bf16[128,2048]{1,0:T(8,128)(2,1)} %param.7) | data formatting | bytes 1048576 | tf_op args[0]
  1.4 1.0 copy.12
  3.5 0.9 collective-permute-done
  5.0 0.7 convolution_convert_fusion.3
  6.2 1.5 %collective-permute-done.1 = bf16[512,512]{1,0:T(8,128)(2,1)S(1)} collective-permute-done((bf16[512,512]{1,0:T(8,128)(2,1)S(1)}, bf16[512,512]{1,0:T(8,128)(2,1)S(1)}, u32[]{:S(2)}, u32[]{:S(2)}) %collective-permute-start.1) | collective-permute-done | bytes 524320 | tf_op jit(solution)/shard_map/ppermute | solution.py:18
  9.1 1.2 multiply_convert_fusion
  10.3 0.7 convolution_convert_fusion.2
  11.4 1.5 %collective-permute-done.2 = bf16[512,512]{1,0:T(8,128)(2,1)S(1)} collective-permute-done((bf16[512,512]{1,0:T(8,128)(2,1)S(1)}, bf16[512,512]{1,0:T(8,128)(2,1)S(1)}, u32[]{:S(2)}, u32[]{:S(2)}) %collective-permute-start.2) | collective-permute-done | bytes 524320 | tf_op jit(solution)/shard_map/ppermute | solution.py:18
  13.0 2.3 %fusion = bf16[1024,512]{1,0:T(8,128)(2,1)} fusion(bf16[1024,512]{1,0:T(8,128)(2,1)S(1)} %multiply_convert_fusion, bf16[1,1024,512]{2,1,0:T(8,128)(2,1)S(1)} %copy-done.4, bf16[512,512]{1,0:T(8,128)(2,1)S(1)} %collective-permute-done.2, bf16[512,512]{1,0:T(8,128)(2,1)S(1)} %convolution_convert_fusion.2), kind=kOutput, calls=%fused_computation.3 | convolution fusion | flops 812908544 | bytes 4194304 | tf_op jit(solution)/shard_map/dot_general | solution.py:78
  15.3 6.2 %all-to-all-start = ((bf16[8,128,512]{2,1,0:T(8,128)(2,1)}), bf16[8,128,512]{2,1,0:T(8,128)(2,1)S(1)}, u32[]{:S(2)}, u32[]{:S(2)}) async-start(bf16[8,128,512]{2,1,0:T(8,128)(2,1)} %bitcast.9), calls=%async_computation | async-start | bytes 2097152 | tf_op jit(solution)/shard_map/all_to_all | solution.py:86
  23.0 25.1 %all-to-all-done = bf16[8,128,512]{2,1,0:T(8,128)(2,1)S(1)} async-done(((bf16[8,128,512]{2,1,0:T(8,128)(2,1)}), bf16[8,128,512]{2,1,0:T(8,128)(2,1)S(1)}, u32[]{:S(2)}, u32[]{:S(2)}) %all-to-all-start) | async-done | bytes 1048608 | tf_op jit(solution)/shard_map/all_to_all | solution.py:86
  49.0 28.6 %all_to_all.15 = bf16[8,256,512]{2,1,0:T(8,128)(2,1)S(1)} all-to-all(bf16[8,256,512]{2,1,0:T(8,128)(2,1)S(1)} %broadcast_select_fusion), channel_id=1, replica_groups=mesh['group'=4,'slot'=8] {'group'}, dimensions={0} | all-to-all | bytes 4194304 | tf_op jit(solution)/shard_map/all_to_all | solution.py:100
  77.6 0.7 fusion.28
  78.3 0.7 fusion.27
  79.0 0.7 fusion.26
  79.7 0.7 fusion.25
  80.5 0.7 fusion.24
  81.2 0.7 fusion.23
  81.9 0.7 fusion.22
  82.7 0.7 fusion.21
  83.4 3.7 %all-to-all-start.2 = ((bf16[8,1,256,512]{3,2,1,0:T(8,128)(2,1)}), bf16[8,1,256,512]{3,2,1,0:T(8,128)(2,1)S(1)}, u32[]{:S(2)}, u32[]{:S(2)}) async-start(bf16[8,1,256,512]{3,2,1,0:T(8,128)(2,1)} %fusion.21), calls=%async_computation.2 | async-start | bytes 4194304 | tf_op jit(solution)/shard_map/all_to_all | solution.py:97
  87.2 0.9 gather_fusion
  88.1 48.0 %all-to-all-done.2 = bf16[8,1,256,512]{3,2,1,0:T(8,128)(2,1)S(1)} async-done(((bf16[8,1,256,512]{3,2,1,0:T(8,128)(2,1)}), bf16[8,1,256,512]{3,2,1,0:T(8,128)(2,1)S(1)}, u32[]{:S(2)}, u32[]{:S(2)}) %all-to-all-start.2) | async-done | bytes 2097184 | tf_op jit(solution)/shard_map/all_to_all | solution.py:97
  136.1 1.2 convolution_convert_fusion.4
  (32 shorter events, 5.6 us)
Async XLA Ops:
  0.0 21.5 %copy-start = (s32[4,8]{1,0:T(4,128)S(1)}, s32[4,8]{1,0:T(4,128)}, u32[]{:S(2)}) copy-start(s32[4,8]{1,0:T(4,128)} %param.12) | copy-start | bytes 388
  0.0 3.1 %copy-start.3 = (bf16[128,512]{1,0:T(8,128)(2,1)S(1)}, bf16[128,512]{1,0:T(8,128)(2,1)}, u32[]{:S(2)}) copy-start(bf16[128,512]{1,0:T(8,128)(2,1)} %param.8) | copy-start | bytes 393220
  0.0 4.5 %copy-start.2 = (bf16[1,1024,512]{2,1,0:T(8,128)(2,1)S(1)}, bf16[1,1024,512]{2,1,0:T(8,128)(2,1)}, u32[]{:S(2)}) copy-start(bf16[1,1024,512]{2,1,0:T(8,128)(2,1)} %param.10) | copy-start | bytes 3145732
  2.5 1.9 %collective-permute-start = (bf16[128,1536]{0,1:T(8,128)(2,1)S(1)}, bf16[128,1536]{0,1:T(8,128)(2,1)S(1)}, u32[]{:S(2)}, u32[]{:S(2)}) collective-permute-start(bf16[128,1536]{0,1:T(8,128)(2,1)S(1)} %pad_maximum_fusion), channel_id=1, source_target_pairs={{0,1},{1,0},{2,3},{3,2},{4,5},{5,4},{6,7},{7,6},{8,9},{9,8},{10,11... | collective-permute-start | bytes 1179656 | tf_op jit(solution)/shard_map/ppermute | solution.py:18
  5.7 2.0 %collective-permute-start.1 = (bf16[512,512]{1,0:T(8,128)(2,1)S(1)}, bf16[512,512]{1,0:T(8,128)(2,1)S(1)}, u32[]{:S(2)}, u32[]{:S(2)}) collective-permute-start(bf16[512,512]{1,0:T(8,128)(2,1)S(1)} %convolution_convert_fusion.3), channel_id=1, source_target_pairs={{0,1},{1,0},{2,3},{3,2},{4,5},{5,4},{6,7},{7,6},{8,9},{9,8},{10,11... | collective-permute-start | bytes 1572872 | tf_op jit(solution)/shard_map/ppermute | solution.py:18
  10.3 2.7 %copy-start.4 = (bf16[1,1024,512]{2,1,0:T(8,128)(2,1)S(1)}, bf16[1,1024,512]{2,1,0:T(8,128)(2,1)}, u32[]{:S(2)}) copy-start(bf16[1,1024,512]{2,1,0:T(8,128)(2,1)} %param.9) | copy-start | bytes 3145732
  11.0 2.0 %collective-permute-start.2 = (bf16[512,512]{1,0:T(8,128)(2,1)S(1)}, bf16[512,512]{1,0:T(8,128)(2,1)S(1)}, u32[]{:S(2)}, u32[]{:S(2)}) collective-permute-start(bf16[512,512]{1,0:T(8,128)(2,1)S(1)} %convolution_convert_fusion.2), channel_id=1, source_target_pairs={{0,1},{1,0},{2,3},{3,2},{4,5},{5,4},{6,7},{7,6},{8,9},{9,8},{10,11... | collective-permute-start | bytes 1572872 | tf_op jit(solution)/shard_map/ppermute | solution.py:18
  15.3 32.8 %all-to-all-start = ((bf16[8,128,512]{2,1,0:T(8,128)(2,1)}), bf16[8,128,512]{2,1,0:T(8,128)(2,1)S(1)}, u32[]{:S(2)}, u32[]{:S(2)}) async-start(bf16[8,128,512]{2,1,0:T(8,128)(2,1)} %bitcast.9), calls=%async_computation | async-start | bytes 2097152 | tf_op jit(solution)/shard_map/all_to_all | solution.py:86
  83.4 3.7 %copy-start.5 = (s32[1,128]{1,0:T(1,128)S(1)}, s32[1,128]{1,0:T(1,128)}, u32[]{:S(2)}) copy-start(s32[1,128]{1,0:T(1,128)} %param.13) | copy-start | bytes 1540
  83.4 3.8 %copy-start.1 = (bf16[128,2048]{1,0:T(8,128)(2,1)S(1)}, bf16[128,2048]{1,0:T(8,128)(2,1)}, u32[]{:S(2)}) copy-start(bf16[128,2048]{1,0:T(8,128)(2,1)} %param.7) | copy-start | bytes 1572868
  83.4 52.7 %all-to-all-start.2 = ((bf16[8,1,256,512]{3,2,1,0:T(8,128)(2,1)}), bf16[8,1,256,512]{3,2,1,0:T(8,128)(2,1)S(1)}, u32[]{:S(2)}, u32[]{:S(2)}) async-start(bf16[8,1,256,512]{3,2,1,0:T(8,128)(2,1)} %fusion.21), calls=%async_computation.2 | async-start | bytes 4194304 | tf_op jit(solution)/shard_map/all_to_all | solution.py:97
